TPU v7x, 512 devices: a whole 4x8x8 slice. The times are simulated.
512 devices in a mesh: sta: 128 (over z_hi, y, x, core), cell: 4 (over z_lo).
Axes of the slice: x: 4, y: 8, z: 8 (z_hi: 2, z_lo: 4; z = z_hi * 4 + z_lo), core: 2. Of those that a mesh axis runs over, the one named last changes fastest.
Arguments:
- sensitivity: bfloat16 [2048, 52, 2048], P('sta', None, 'cell'), may hold values from -0.01953125 to 0.01953125
- footprint: int32 [128, 52], P('sta'), may hold values from 0 to 63, as said below
- linked: int32 [128, 9], P('sta'), may hold values from 0 to 1, as said below
- smooth_x: bfloat16 [16, 16], replicated, may hold values from 0 to 8, as said below
- smooth_y: bfloat16 [64, 64], replicated, may hold values from 0 to 8, as said below
- smooth_z: bfloat16 [128, 128], replicated, may hold values from 0 to 8, as said below
Outputs:
- band: float32 [2048, 144], P('sta', 'cell')
Inputs may be any that keep to these rules, and one draw needn't show every extreme that they name: `footprint`: within a row the 52 tiles are different. linked[b, 4] is 1, and linked[b, 4 + k] equals linked[(b + k) mod the number of row blocks, 4 - k] for 1 <= k <= 4. `smooth_x`: Symmetric, with positive entries. `smooth_y`: Symmetric, with positive entries. `smooth_z`: Symmetric, with positive entries.
All inputs are finite; a program needn't handle non-finite values.
Results may differ from a plain program's by a relative error of at most 0.005.
Values may be sent and summed in bfloat16 or wider, within the bound.
A program may use at most 64 MiB of HBM per device.

v0:
```python
import math
import jax
import jax.numpy as jnp
from jax import lax
from jax.sharding import PartitionSpec as P

TILE = 16
HALF = 4
TILES = 64
BAND = 9


def from_behind(block, axis, distance):
    devices = range(lax.axis_size(axis))
    route = [((i - distance) % len(devices), i) for i in devices]
    return lax.ppermute(block, axis, route)


def in_blocks(array, dim, size):
    before, after = (array.shape[:dim], array.shape[dim + 1 :])
    return jnp.moveaxis(array.reshape(*before, size, -1, *after), dim, 0)


def sent_and_summed(array, axis, dim):
    blocks = in_blocks(array, dim, lax.axis_size(axis))
    arrived = lax.all_to_all(blocks, axis, split_axis=0, concat_axis=0, tiled=True)
    return arrived.sum(axis=0)


def spread_tiles(values, foot_tiles):
    onehot = (foot_tiles[:, None] == jnp.arange(TILES, dtype=jnp.int32)[None, :]).astype(
        jnp.bfloat16
    )
    placed = jnp.einsum("rfk,ft->rtk", values, onehot, preferred_element_type=jnp.float32)
    return placed.astype(jnp.bfloat16)


def smooth_depth(block, smooth_z):
    row_count, tile_count, slab_width = block.shape
    depth_cells = smooth_z.shape[0]
    grid_field = block.reshape(row_count, tile_count, depth_cells, slab_width // depth_cells)
    smoothed = jnp.einsum("rtzc,wz->rtwc", grid_field, smooth_z, preferred_element_type=jnp.float32)
    return smoothed.astype(jnp.bfloat16).reshape(row_count, tile_count, slab_width)


def smooth_plane(field_rows, smooth_x, smooth_y):
    row_count, tile_count, slab_width = field_rows.shape
    cells_across = smooth_x.shape[0]
    blocks_along = tile_count // cells_across
    group_rows = math.gcd(row_count, 4)
    y_kernel = smooth_y.reshape(blocks_along, TILE, blocks_along, TILE)

    def smooth_group(row_group):
        grid_field = row_group.reshape(
            group_rows, cells_across, blocks_along, slab_width // TILE, TILE
        )
        across = jnp.einsum(
            "rxbzc,vx->rvbzc", grid_field, smooth_x, preferred_element_type=jnp.float32
        ).astype(jnp.bfloat16)
        along = jnp.einsum(
            "rxbzc,ekbc->rxezk", across, y_kernel, preferred_element_type=jnp.float32
        ).astype(jnp.bfloat16)
        return along.reshape(group_rows, tile_count, slab_width)

    grouped = field_rows.reshape(row_count // group_rows, group_rows, tile_count, slab_width)
    return lax.map(smooth_group, grouped).reshape(row_count, tile_count, slab_width)


def pair_tile(smoothed, values, foot_tiles):
    row_count = smoothed.shape[0]
    picked = jnp.take(smoothed, foot_tiles, axis=1).reshape(row_count, -1)
    partner = values.reshape(values.shape[0], -1)
    return lax.dot_general(
        picked, partner, (((1,), (1,)), ((), ())), preferred_element_type=jnp.float32
    )


def body(sensitivity, footprint, linked, smooth_x, smooth_y, smooth_z):
    own_tiles = footprint[0]
    depth_rows = lax.all_to_all(
        smooth_depth(
            lax.all_to_all(sensitivity, "cell", split_axis=1, concat_axis=2, tiled=True), smooth_z
        ),
        "cell",
        split_axis=2,
        concat_axis=1,
        tiled=True,
    )
    grid_rows = spread_tiles(depth_rows, own_tiles)
    smoothed = smooth_plane(grid_rows, smooth_x, smooth_y)
    pair_flags = linked[0]

    def masked_tile(values, foot_tiles, flag):
        return pair_tile(smoothed, values, foot_tiles) * flag.astype(jnp.float32)

    band_parts = [None] * BAND
    band_parts[HALF] = masked_tile(sensitivity, own_tiles, pair_flags[HALF])
    carried = (sensitivity, footprint)
    for offset in range(1, HALF + 1):
        carried = from_behind((carried[0], carried[1]), "sta", 1)
        band_parts[HALF - offset] = masked_tile(
            carried[0], carried[1][0], pair_flags[HALF - offset]
        )
    for offset in range(1, HALF + 1):
        band_parts[HALF + offset] = from_behind(band_parts[HALF - offset].T, "sta", -offset)
    partial_band = jnp.concatenate(band_parts, axis=1)
    return sent_and_summed(partial_band, "cell", 1)


def solution(mesh):
    return jax.shard_map(
        body,
        mesh=mesh,
        in_specs=(P("sta", None, "cell"), P("sta", None), P("sta", None), P(), P(), P()),
        out_specs=P("sta", "cell"),
        check_vma=False,
    )
```

profile of v0, /device:TPU:62, one launch (start us, length us, event | category | flops | bytes accessed | tf_op | source)
XLA Modules:
  0.0 227.8 jit_solution(7614213136167638222)
XLA Ops:
  0.0 7.4 %all-to-all-start = ((bf16[16,52,512]{2,0,1:T(8,128)(2,1)}), bf16[16,52,512]{2,0,1:T(8,128)(2,1)S(1)}, u32[]{:S(2)}, u32[]{:S(2)}) async-start(bf16[16,52,512]{2,0,1:T(8,128)(2,1)} %param.10), calls=%async_computation | async-start | bytes 1703936 | tf_op jit(solution)/shard_map/all_to_all | solution.py:82
  7.4 1.9 collective-permute-start.4
  9.3 7.4 %collective-permute-start = (s32[1,52]{1,0:T(1,128)}, s32[1,52]{1,0:T(1,128)S(1)}, u32[]{:S(2)}, u32[]{:S(2)}) collective-permute-start(s32[1,52]{1,0:T(1,128)} %param.11), channel_id=1, source_target_pairs={{508,0},{0,4},{4,8},{8,12},{12,16},{16,20},{20,24},{24,28},{28,32}... | collective-permute-start | bytes 632 | tf_op jit(solution)/shard_map/ppermute | solution.py:16
  23.5 9.2 %collective-permute-start.1 = (s32[1,52]{1,0:T(1,128)S(1)}, s32[1,52]{1,0:T(1,128)S(1)}, u32[]{:S(2)}, u32[]{:S(2)}) collective-permute-start(s32[1,52]{1,0:T(1,128)S(1)} %collective-permute-done), channel_id=1, source_target_pairs={{508,0},{0,4},{4,8},{8,12},{12,16},{16,20},{20,24},{24,28},{28,32}... | collective-permute-start | bytes 632 | tf_op jit(solution)/shard_map/ppermute | solution.py:16
  33.5 15.7 %collective-permute-start.2 = (s32[1,52]{1,0:T(1,128)S(1)}, s32[1,52]{1,0:T(1,128)S(1)}, u32[]{:S(2)}, u32[]{:S(2)}) collective-permute-start(s32[1,52]{1,0:T(1,128)S(1)} %collective-permute-done.1), channel_id=1, source_target_pairs={{508,0},{0,4},{4,8},{8,12},{12,16},{16,20},{20,24},{24,28},{28,32}... | collective-permute-start | bytes 632 | tf_op jit(solution)/shard_map/ppermute | solution.py:16
  49.2 12.3 %collective-permute-start.5 = (bf16[16,52,512]{2,0,1:T(8,128)(2,1)S(1)}, bf16[16,52,512]{2,0,1:T(8,128)(2,1)}, u32[]{:S(2)}, u32[]{:S(2)}) collective-permute-start(bf16[16,52,512]{2,0,1:T(8,128)(2,1)S(1)} %collective-permute-done.4), channel_id=1, source_target_pairs={{508,0},{0,4},{4,8},{8,12},{12,16},{16,20},{20,24},{24,28},{28,32}... | collective-permute-start | bytes 2555912 | tf_op jit(solution)/shard_map/ppermute | solution.py:16
  62.2 6.1 %reshape.56 = bf16[16,13,128,16]{3,2,1,0:T(8,128)(2,1)} reshape(bf16[16,13,4,512]{3,2,1,0:T(4,128)(2,1)S(1)} %bitcast.140) | data formatting | bytes 1703936 | tf_op jit(solution)/shard_map/reshape | solution.py:41
  68.3 4.8 %fusion.5 = bf16[16,13,128,16]{2,3,1,0:T(8,128)(2,1)S(1)} fusion(bf16[16,13,128,16]{3,2,1,0:T(8,128)(2,1)} %reshape.56, bf16[128,128]{1,0:T(8,128)(2,1)S(1)} %copy-done), kind=kOutput, calls=%fused_computation.16 | convolution fusion | flops 109477888 | bytes 1736704 | tf_op jit(solution)/shard_map/rtzc,wz->rtwc/dot_general | solution.py:42
  73.2 12.5 %copy.60 = bf16[16,13,128,16]{0,1,3,2:T(8,128)(2,1)} copy(bf16[16,13,128,16]{2,3,1,0:T(8,128)(2,1)S(1)} %fusion.5) | data formatting | bytes 1703936 | tf_op jit(solution)/shard_map/reshape | solution.py:43
  85.7 8.3 %reshape.128 = bf16[4,2,53248]{2,1,0:T(2,128)(2,1)} reshape(bf16[2048,13,16]{2,1,0:T(8,128)(2,1)} %bitcast.135) | data formatting | bytes 1703936
  94.0 5.8 %all-to-all-start.1 = ((bf16[4,2,53248]{2,1,0:T(2,128)(2,1)}), bf16[4,2,53248]{2,1,0:T(2,128)(2,1)S(1)}, u32[]{:S(2)}, u32[]{:S(2)}) async-start(bf16[4,2,53248]{2,1,0:T(2,128)(2,1)} %reshape.128), calls=%async_computation.1 | async-start | bytes 1703936 | tf_op jit(solution)/shard_map/all_to_all | solution.py:80
  99.9 1.9 collective-permute-start.3
  101.8 2.1 collective-permute-start.6
  104.8 16.7 %all-to-all-done.1 = bf16[4,2,53248]{2,1,0:T(2,128)(2,1)S(1)} async-done(((bf16[4,2,53248]{2,1,0:T(2,128)(2,1)}), bf16[4,2,53248]{2,1,0:T(2,128)(2,1)S(1)}, u32[]{:S(2)}, u32[]{:S(2)}) %all-to-all-start.1) | async-done | bytes 852000 | tf_op jit(solution)/shard_map/all_to_all | solution.py:80
  121.5 7.7 %reshape.129 = bf16[2048,13,16]{2,1,0:T(8,128)(2,1)} reshape(bf16[4,2,53248]{2,1,0:T(2,128)(2,1)S(1)} %all-to-all-done.1) | data formatting | bytes 1703936
  129.3 9.3 %copy.61 = bf16[16,13,4,512]{3,2,0,1:T(4,128)(2,1)S(1)} copy(bf16[16,13,4,512]{0,1,3,2:T(8,128)(2,1)} %bitcast.136) | data formatting | bytes 1703936 | tf_op jit(solution)/shard_map/all_to_all | solution.py:80
  138.8 2.3 convolution_convert_fusion.1
  141.0 1.9 collective-permute-start.7
  143.0 40.5 %while.10 = (s32[]{:T(128)}, bf16[4,4,64,512]{3,2,1,0:T(8,128)(2,1)}, bf16[4,4,64,512]{3,2,1,0:T(8,128)(2,1)}, bf16[16,16]{1,0:T(8,128)(2,1)S(1)}, bf16[4,16,4,16]{3,1,2,0:T(8,128)(2,1)S(1)}, /*index=5*/s32[]{:T(128)}) while((s32[]{:T(128)}, bf16[4,4,64,512]{3,2,1,0:T(8,128)(2,1)}, bf16[4,4,64,512]{3,2,1,0:T(8,128)(2,1)}, ...), condition=%wide.region_1.2_spmd, body=%wide.region_0.1_spmd.sunk | while | flops 21233664 | bytes 4203593 | solution.py:66
  148.8 3.6 %broadcast_in_dim.31 = bf16[1,4,64,512]{3,2,1,0:T(8,128)(2,1)S(1)} reshape(bf16[4,16,4,32,16]{4,3,2,1,0:T(8,128)(2,1)S(1)} %copy.80) | data formatting | bytes 524288 | tf_op jit(solution)/shard_map/while/body/jit(dynamic_update_index_in_dim)/broadcast_in_dim | solution.py:66
  158.9 3.6 %broadcast_in_dim.31 = bf16[1,4,64,512]{3,2,1,0:T(8,128)(2,1)S(1)} reshape(bf16[4,16,4,32,16]{4,3,2,1,0:T(8,128)(2,1)S(1)} %copy.80) | data formatting | bytes 524288 | tf_op jit(solution)/shard_map/while/body/jit(dynamic_update_index_in_dim)/broadcast_in_dim | solution.py:66
  169.0 3.6 %broadcast_in_dim.31 = bf16[1,4,64,512]{3,2,1,0:T(8,128)(2,1)S(1)} reshape(bf16[4,16,4,32,16]{4,3,2,1,0:T(8,128)(2,1)S(1)} %copy.80) | data formatting | bytes 524288 | tf_op jit(solution)/shard_map/while/body/jit(dynamic_update_index_in_dim)/broadcast_in_dim | solution.py:66
  179.2 3.6 %broadcast_in_dim.31 = bf16[1,4,64,512]{3,2,1,0:T(8,128)(2,1)S(1)} reshape(bf16[4,16,4,32,16]{4,3,2,1,0:T(8,128)(2,1)S(1)} %copy.80) | data formatting | bytes 524288 | tf_op jit(solution)/shard_map/while/body/jit(dynamic_update_index_in_dim)/broadcast_in_dim | solution.py:66
  183.5 1.8 copy.62
  186.6 1.7 fusion.9
  188.3 1.9 collective-permute-start.10
  192.6 1.9 collective-permute-start.9
  195.1 1.7 fusion.7
  196.8 3.7 %collective-permute-start.8 = (f32[16,16]{1,0:T(8,128)S(1)}, f32[16,16]{1,0:T(8,128)S(1)}, u32[]{:S(2)}, u32[]{:S(2)}) collective-permute-start(f32[16,16]{1,0:T(8,128)S(1)} %bitcast.145), channel_id=1, source_target_pairs={{4,0},{8,4},{12,8},{16,12},{20,16},{24,20},{28,24},{32,28},{36,32}... | collective-permute-start | bytes 3080 | tf_op jit(solution)/shard_map/ppermute | solution.py:16
  202.9 1.9 collective-permute-start.11
  207.4 10.1 %collective-permute-done.11 = f32[16,16]{1,0:T(8,128)S(1)} collective-permute-done((f32[16,16]{1,0:T(8,128)S(1)}, f32[16,16]{1,0:T(8,128)S(1)}, u32[]{:S(2)}, u32[]{:S(2)}) %collective-permute-start.11) | collective-permute-done | bytes 1056 | tf_op jit(solution)/shard_map/ppermute | solution.py:16
  217.8 8.1 %all_to_all.38 = f32[4,1,576]{2,1,0:T(1,128)S(1)} all-to-all(f32[4,1,576]{2,1,0:T(1,128)S(1)} %reshape.130), channel_id=1, replica_groups=mesh['sta'=128,'cell'=4] {'cell'}, dimensions={0} | all-to-all | bytes 18432 | tf_op jit(solution)/shard_map/all_to_all | solution.py:26
  (89 shorter events, 43.4 us)
Async XLA Ops:
  0.0 68.3 %copy-start = (bf16[128,128]{1,0:T(8,128)(2,1)S(1)}, bf16[128,128]{1,0:T(8,128)(2,1)}, u32[]{:S(2)}) copy-start(bf16[128,128]{1,0:T(8,128)(2,1)} %param.15) | copy-start | bytes 98308
  0.0 61.5 %all-to-all-start = ((bf16[16,52,512]{2,0,1:T(8,128)(2,1)}), bf16[16,52,512]{2,0,1:T(8,128)(2,1)S(1)}, u32[]{:S(2)}, u32[]{:S(2)}) async-start(bf16[16,52,512]{2,0,1:T(8,128)(2,1)} %param.10), calls=%async_computation | async-start | bytes 1703936 | tf_op jit(solution)/shard_map/all_to_all | solution.py:82
  7.4 41.8 %collective-permute-start.4 = (bf16[16,52,512]{2,0,1:T(8,128)(2,1)}, bf16[16,52,512]{2,0,1:T(8,128)(2,1)S(1)}, u32[]{:S(2)}, u32[]{:S(2)}) collective-permute-start(bf16[16,52,512]{2,0,1:T(8,128)(2,1)} %param.10), channel_id=1, source_target_pairs={{508,0},{0,4},{4,8},{8,12},{12,16},{16,20},{20,24},{24,28},{28,32}... | collective-permute-start | bytes 2555912 | tf_op jit(solution)/shard_map/ppermute | solution.py:16
  9.3 14.2 %collective-permute-start = (s32[1,52]{1,0:T(1,128)}, s32[1,52]{1,0:T(1,128)S(1)}, u32[]{:S(2)}, u32[]{:S(2)}) collective-permute-start(s32[1,52]{1,0:T(1,128)} %param.11), channel_id=1, source_target_pairs={{508,0},{0,4},{4,8},{8,12},{12,16},{16,20},{20,24},{24,28},{28,32}... | collective-permute-start | bytes 632 | tf_op jit(solution)/shard_map/ppermute | solution.py:16
  23.5 10.0 %collective-permute-start.1 = (s32[1,52]{1,0:T(1,128)S(1)}, s32[1,52]{1,0:T(1,128)S(1)}, u32[]{:S(2)}, u32[]{:S(2)}) collective-permute-start(s32[1,52]{1,0:T(1,128)S(1)} %collective-permute-done), channel_id=1, source_target_pairs={{508,0},{0,4},{4,8},{8,12},{12,16},{16,20},{20,24},{24,28},{28,32}... | collective-permute-start | bytes 632 | tf_op jit(solution)/shard_map/ppermute | solution.py:16
  33.5 66.4 %collective-permute-start.2 = (s32[1,52]{1,0:T(1,128)S(1)}, s32[1,52]{1,0:T(1,128)S(1)}, u32[]{:S(2)}, u32[]{:S(2)}) collective-permute-start(s32[1,52]{1,0:T(1,128)S(1)} %collective-permute-done.1), channel_id=1, source_target_pairs={{508,0},{0,4},{4,8},{8,12},{12,16},{16,20},{20,24},{24,28},{28,32}... | collective-permute-start | bytes 632 | tf_op jit(solution)/shard_map/ppermute | solution.py:16
  49.2 24.0 %copy-start.3 = (bf16[16,52,512]{2,0,1:T(8,128)(2,1)}, bf16[16,52,512]{2,0,1:T(8,128)(2,1)S(1)}, u32[]{:S(2)}) copy-start(bf16[16,52,512]{2,0,1:T(8,128)(2,1)S(1)} %collective-permute-done.4) | copy-start | bytes 2555908
  49.2 52.6 %collective-permute-start.5 = (bf16[16,52,512]{2,0,1:T(8,128)(2,1)S(1)}, bf16[16,52,512]{2,0,1:T(8,128)(2,1)}, u32[]{:S(2)}, u32[]{:S(2)}) collective-permute-start(bf16[16,52,512]{2,0,1:T(8,128)(2,1)S(1)} %collective-permute-done.4), channel_id=1, source_target_pairs={{508,0},{0,4},{4,8},{8,12},{12,16},{16,20},{20,24},{24,28},{28,32}... | collective-permute-start | bytes 2555912 | tf_op jit(solution)/shard_map/ppermute | solution.py:16
  94.0 27.5 %all-to-all-start.1 = ((bf16[4,2,53248]{2,1,0:T(2,128)(2,1)}), bf16[4,2,53248]{2,1,0:T(2,128)(2,1)S(1)}, u32[]{:S(2)}, u32[]{:S(2)}) async-start(bf16[4,2,53248]{2,1,0:T(2,128)(2,1)} %reshape.128), calls=%async_computation.1 | async-start | bytes 1703936 | tf_op jit(solution)/shard_map/all_to_all | solution.py:80
  99.9 4.9 %collective-permute-start.3 = (s32[1,52]{1,0:T(1,128)S(1)}, s32[1,52]{1,0:T(1,128)S(1)}, u32[]{:S(2)}, u32[]{:S(2)}) collective-permute-start(s32[1,52]{1,0:T(1,128)S(1)} %collective-permute-done.2), channel_id=1, source_target_pairs={{508,0},{0,4},{4,8},{8,12},{12,16},{16,20},{20,24},{24,28},{28,32}... | collective-permute-start | bytes 632 | tf_op jit(solution)/shard_map/ppermute | solution.py:16
  101.8 39.2 %collective-permute-start.6 = (bf16[16,52,512]{2,0,1:T(8,128)(2,1)}, bf16[16,52,512]{2,0,1:T(8,128)(2,1)}, u32[]{:S(2)}, u32[]{:S(2)}) collective-permute-start(bf16[16,52,512]{2,0,1:T(8,128)(2,1)} %collective-permute-done.5), channel_id=1, source_target_pairs={{508,0},{0,4},{4,8},{8,12},{12,16},{16,20},{20,24},{24,28},{28,32}... | collective-permute-start | bytes 2555912 | tf_op jit(solution)/shard_map/ppermute | solution.py:16
  129.3 9.5 %copy-start.2 = (s32[1,52]{1,0:T(1,128)S(1)}, s32[1,52]{1,0:T(1,128)}, u32[]{:S(2)}) copy-start(s32[1,52]{1,0:T(1,128)} %param.11) | copy-start | bytes 628
  129.3 13.7 %copy-start.1 = (bf16[16,16]{1,0:T(8,128)(2,1)S(1)}, bf16[16,16]{1,0:T(8,128)(2,1)}, u32[]{:S(2)}) copy-start(bf16[16,16]{1,0:T(8,128)(2,1)} %param.13) | copy-start | bytes 1540
  141.0 60.1 %collective-permute-start.7 = (bf16[16,52,512]{2,0,1:T(8,128)(2,1)}, bf16[16,52,512]{2,0,1:T(8,128)(2,1)}, u32[]{:S(2)}, u32[]{:S(2)}) collective-permute-start(bf16[16,52,512]{2,0,1:T(8,128)(2,1)} %collective-permute-done.6), channel_id=1, source_target_pairs={{508,0},{0,4},{4,8},{8,12},{12,16},{16,20},{20,24},{24,28},{28,32}... | collective-permute-start | bytes 2555912 | tf_op jit(solution)/shard_map/ppermute | solution.py:16
  188.3 18.5 %collective-permute-start.10 = (f32[16,16]{1,0:T(8,128)S(1)}, f32[16,16]{1,0:T(8,128)S(1)}, u32[]{:S(2)}, u32[]{:S(2)}) collective-permute-start(f32[16,16]{1,0:T(8,128)S(1)} %bitcast.143), channel_id=1, source_target_pairs={{12,0},{16,4},{20,8},{24,12},{28,16},{32,20},{36,24},{40,28},{44,3... | collective-permute-start | bytes 3080 | tf_op jit(solution)/shard_map/ppermute | solution.py:16
  192.6 14.9 %collective-permute-start.9 = (f32[16,16]{1,0:T(8,128)S(1)}, f32[16,16]{1,0:T(8,128)S(1)}, u32[]{:S(2)}, u32[]{:S(2)}) collective-permute-start(f32[16,16]{1,0:T(8,128)S(1)} %bitcast.144), channel_id=1, source_target_pairs={{8,0},{12,4},{16,8},{20,12},{24,16},{28,20},{32,24},{36,28},{40,32... | collective-permute-start | bytes 3080 | tf_op jit(solution)/shard_map/ppermute | solution.py:16
  196.8 10.6 %collective-permute-start.8 = (f32[16,16]{1,0:T(8,128)S(1)}, f32[16,16]{1,0:T(8,128)S(1)}, u32[]{:S(2)}, u32[]{:S(2)}) collective-permute-start(f32[16,16]{1,0:T(8,128)S(1)} %bitcast.145), channel_id=1, source_target_pairs={{4,0},{8,4},{12,8},{16,12},{20,16},{24,20},{28,24},{32,28},{36,32}... | collective-permute-start | bytes 3080 | tf_op jit(solution)/shard_map/ppermute | solution.py:16
  202.9 14.6 %collective-permute-start.11 = (f32[16,16]{1,0:T(8,128)S(1)}, f32[16,16]{1,0:T(8,128)S(1)}, u32[]{:S(2)}, u32[]{:S(2)}) collective-permute-start(f32[16,16]{1,0:T(8,128)S(1)} %bitcast.146), channel_id=1, source_target_pairs={{16,0},{20,4},{24,8},{28,12},{32,16},{36,20},{40,24},{44,28},{48,3... | collective-permute-start | bytes 3080 | tf_op jit(solution)/shard_map/ppermute | solution.py:16
where the time goes:
time: 229 us; the launch traced here: 228 us
  local copies, waits for them, and re-layouts  90 us (39%)
  starting transfers between devices  75.1 us (33%)
  waiting for transfers between devices  29 us (13%)
  matrix products  19.2 us (8%)
  blocking collectives  8.13 us (4%)
  between operations  3.47 us (2%)
  other arithmetic  2.69 us (1%)
    ppermute x12, starting transfers between devices, from_behind(): return lax.ppermute(block, axis, route)  61.9 us
    all_to_all x1, waiting for transfers between devices, body(): lax.all_to_all(smooth_depth(lax.all_to_all(sensitivity, 'cell', split_axi...  16.7 us
    unnamed x12, local copies, waits for them, and re-layouts  16.3 us
    broadcast_in_dim x4, local copies, waits for them, and re-layouts, smooth_plane(): lax.map(smooth_group, grouped).reshape(row_count, tile_count, slab_width)  14.3 us
    reshape x1, local copies, waits for them, and re-layouts, smooth_depth(): smoothed.astype(jnp.bfloat16).reshape(row_count, tile_count, slab_width)  12.5 us
    ppermute x12, waiting for transfers between devices, from_behind(): return lax.ppermute(block, axis, route)  12.3 us
    reshape x8, local copies, waits for them, and re-layouts, smooth_group(): row_group.reshape(group_rows, cells_across, blocks_along, slab_width // T...  11.4 us
    all_to_all x2, local copies, waits for them, and re-layouts, body(): lax.all_to_all(smooth_depth(lax.all_to_all(sensitivity, 'cell', split_axi...  9.47 us
  transfers between devices with their start and end apart: 14, of which 5 were waited for; matrix products, arithmetic and copies ran while one was open for 48% of the time, Pallas kernels for 0%

commit v1 on v0

--- a/solution.py
+++ b/solution.py
@@ -77,15 +77,13 @@
 
 def body(sensitivity, footprint, linked, smooth_x, smooth_y, smooth_z):
     own_tiles = footprint[0]
-    depth_rows = lax.all_to_all(
-        smooth_depth(
-            lax.all_to_all(sensitivity, "cell", split_axis=1, concat_axis=2, tiled=True), smooth_z
-        ),
-        "cell",
-        split_axis=2,
-        concat_axis=1,
-        tiled=True,
+    part = smooth_depth(
+        lax.all_to_all(sensitivity, "cell", split_axis=1, concat_axis=2, tiled=True), smooth_z
     )
+    peers = lax.axis_size("cell")
+    shards = jnp.stack(jnp.split(part, peers, axis=2), axis=0)
+    shards = lax.all_to_all(shards, "cell", split_axis=0, concat_axis=0)
+    depth_rows = jnp.concatenate(shards, axis=1)
     grid_rows = spread_tiles(depth_rows, own_tiles)
     smoothed = smooth_plane(grid_rows, smooth_x, smooth_y)
     pair_flags = linked[0]

time: 229 us -> 221 us (0.965)
  local copies, waits for them, and re-layouts: 90 us -> 69.3 us
  waiting for transfers between devices: 29 us -> 38.2 us
  blocking collectives: 8.13 us -> 11.7 us
    unnamed x12, local copies, waits for them, and re-layouts: 16.3 us -> 0.21 us
    all_to_all x2 -> x0, local copies, waits for them, and re-layouts: 9.47 us -> none  [body(): lax.all_to_all(smooth_depth(lax.all_to_all(sensitivity, 'cell', split_axi...]
    ppermute x12, waiting for transfers between devices: 12.3 us -> 21.5 us  [from_behind(): return lax.ppermute(block, axis, route)]
    convert_element_type x0 -> x1, local copies, waits for them, and re-layouts: none -> 5.08 us  [smooth_depth(): smoothed.astype(jnp.bfloat16).reshape(row_count, tile_count, slab_width)]
    all_to_all x1, blocking collectives: 8.13 us -> 11.7 us  [sent_and_summed(): lax.all_to_all(blocks, axis, split_axis=0, concat_axis=0, tiled=True)]
  transfers between devices with their start and end apart: 14 -> 14, of which waited for: 5 -> 6; matrix products, arithmetic and copies ran while one was open for 48% -> 40% of each run, Pallas kernels for 0% -> 0%
where the time goes in v1:
time: 221 us; the launch traced here: 220 us
  starting transfers between devices  75.5 us (34%)
  local copies, waits for them, and re-layouts  69.3 us (31%)
  waiting for transfers between devices  38.2 us (17%)
  matrix products  18.1 us (8%)
  blocking collectives  11.7 us (5%)
  other arithmetic  3.71 us (2%)
  between operations  3.26 us (1%)
    ppermute x12, starting transfers between devices, from_behind(): return lax.ppermute(block, axis, route)  62.1 us
    ppermute x12, waiting for transfers between devices, from_behind(): return lax.ppermute(block, axis, route)  21.5 us
    all_to_all x1, waiting for transfers between devices, body(): shards = lax.all_to_all(shards, 'cell', split_axis=0, concat_axis=0)  16.7 us
    broadcast_in_dim x4, local copies, waits for them, and re-layouts, smooth_plane(): lax.map(smooth_group, grouped).reshape(row_count, tile_count, slab_width)  14.3 us
    reshape x1, local copies, waits for them, and re-layouts, smooth_depth(): smoothed.astype(jnp.bfloat16).reshape(row_count, tile_count, slab_width)  12.3 us
    all_to_all x1, blocking collectives, sent_and_summed(): lax.all_to_all(blocks, axis, split_axis=0, concat_axis=0, tiled=True)  11.7 us
    reshape x8, local copies, waits for them, and re-layouts, smooth_group(): row_group.reshape(group_rows, cells_across, blocks_along, slab_width // T...  11.4 us
    dot_general x5, matrix products, pair_tile(): lax.dot_general(picked, partner, (((1,), (1,)), ((), ())), preferred_elem...  7.46 us
  transfers between devices with their start and end apart: 14, of which 6 were waited for; matrix products, arithmetic and copies ran while one was open for 40% of the time, Pallas kernels for 0%

profile of v1, /device:TPU:62, one launch (start us, length us, event | category | flops | bytes accessed | tf_op | source)
XLA Modules:
  0.0 220.1 jit_solution(9820732436093392911)
XLA Ops:
  0.0 7.4 %all-to-all-start = ((bf16[16,52,512]{2,0,1:T(8,128)(2,1)}), bf16[16,52,512]{2,0,1:T(8,128)(2,1)S(1)}, u32[]{:S(2)}, u32[]{:S(2)}) async-start(bf16[16,52,512]{2,0,1:T(8,128)(2,1)} %param.10), calls=%async_computation | async-start | bytes 1703936 | tf_op jit(solution)/shard_map/all_to_all | solution.py:81
  7.4 1.9 collective-permute-start.4
  9.3 7.4 %collective-permute-start = (s32[1,52]{1,0:T(1,128)}, s32[1,52]{1,0:T(1,128)S(1)}, u32[]{:S(2)}, u32[]{:S(2)}) collective-permute-start(s32[1,52]{1,0:T(1,128)} %param.11), channel_id=1, source_target_pairs={{508,0},{0,4},{4,8},{8,12},{12,16},{16,20},{20,24},{24,28},{28,32}... | collective-permute-start | bytes 632 | tf_op jit(solution)/shard_map/ppermute | solution.py:16
  23.3 9.4 %collective-permute-start.1 = (s32[1,52]{1,0:T(1,128)S(1)}, s32[1,52]{1,0:T(1,128)S(1)}, u32[]{:S(2)}, u32[]{:S(2)}) collective-permute-start(s32[1,52]{1,0:T(1,128)S(1)} %collective-permute-done), channel_id=1, source_target_pairs={{508,0},{0,4},{4,8},{8,12},{12,16},{16,20},{20,24},{24,28},{28,32}... | collective-permute-start | bytes 632 | tf_op jit(solution)/shard_map/ppermute | solution.py:16
  33.5 15.7 %collective-permute-start.2 = (s32[1,52]{1,0:T(1,128)S(1)}, s32[1,52]{1,0:T(1,128)S(1)}, u32[]{:S(2)}, u32[]{:S(2)}) collective-permute-start(s32[1,52]{1,0:T(1,128)S(1)} %collective-permute-done.1), channel_id=1, source_target_pairs={{508,0},{0,4},{4,8},{8,12},{12,16},{16,20},{20,24},{24,28},{28,32}... | collective-permute-start | bytes 632 | tf_op jit(solution)/shard_map/ppermute | solution.py:16
  49.2 12.3 %collective-permute-start.5 = (bf16[16,52,512]{2,0,1:T(8,128)(2,1)S(1)}, bf16[16,52,512]{2,0,1:T(8,128)(2,1)}, u32[]{:S(2)}, u32[]{:S(2)}) collective-permute-start(bf16[16,52,512]{2,0,1:T(8,128)(2,1)S(1)} %collective-permute-done.4), channel_id=1, source_target_pairs={{508,0},{0,4},{4,8},{8,12},{12,16},{16,20},{20,24},{24,28},{28,32}... | collective-permute-start | bytes 2555912 | tf_op jit(solution)/shard_map/ppermute | solution.py:16
  62.2 6.1 %reshape.62 = bf16[16,13,128,16]{3,2,1,0:T(8,128)(2,1)} reshape(bf16[16,13,4,512]{3,2,1,0:T(4,128)(2,1)S(1)} %bitcast.146) | data formatting | bytes 1703936 | tf_op jit(solution)/shard_map/reshape | solution.py:41
  68.3 4.8 %fusion.5 = bf16[16,13,128,16]{2,3,1,0:T(8,128)(2,1)S(1)} fusion(bf16[16,13,128,16]{3,2,1,0:T(8,128)(2,1)} %reshape.62, bf16[128,128]{1,0:T(8,128)(2,1)S(1)} %copy-done), kind=kOutput, calls=%fused_computation.16 | convolution fusion | flops 109477888 | bytes 1736704 | tf_op jit(solution)/shard_map/rtzc,wz->rtwc/dot_general | solution.py:42
  73.1 5.1 %copy.36 = bf16[16,13,128,16]{3,2,0,1:T(8,128)(2,1)} copy(bf16[16,13,128,16]{2,3,1,0:T(8,128)(2,1)S(1)} %fusion.5) | data formatting | bytes 1703936 | tf_op jit(solution)/shard_map/convert_element_type | solution.py:43
  78.2 12.3 %reshape.63 = bf16[16,13,2048]{2,0,1:T(8,128)(2,1)S(1)} reshape(bf16[16,13,128,16]{3,2,0,1:T(8,128)(2,1)} %copy.36) | data formatting | bytes 1703936 | tf_op jit(solution)/shard_map/reshape | solution.py:43
  91.7 6.0 %all-to-all-start.1 = ((bf16[4,16,13,512]{3,1,2,0:T(8,128)(2,1)}), bf16[4,16,13,512]{3,1,2,0:T(8,128)(2,1)S(1)}, u32[]{:S(2)}, u32[]{:S(2)}) async-start(bf16[4,16,13,512]{3,1,2,0:T(8,128)(2,1)} %pad_maximum_fusion), calls=%async_computation.1 | async-start | bytes 1703936 | tf_op jit(solution)/shard_map/all_to_all | solution.py:85
  97.7 1.9 collective-permute-start.3
  99.7 1.9 collective-permute-start.6
  102.6 16.7 %all-to-all-done.1 = bf16[4,16,13,512]{3,1,2,0:T(8,128)(2,1)S(1)} async-done(((bf16[4,16,13,512]{3,1,2,0:T(8,128)(2,1)}), bf16[4,16,13,512]{3,1,2,0:T(8,128)(2,1)S(1)}, u32[]{:S(2)}, u32[]{:S(2)}) %all-to-all-start.1) | async-done | bytes 852000 | tf_op jit(solution)/shard_map/all_to_all | solution.py:85
  119.4 2.3 %convolution_convert_fusion.1 = bf16[64,16,512]{2,0,1:T(8,128)(2,1)} fusion(bf16[16,52,512]{2,0,1:T(8,128)(2,1)S(1)} %bitcast.144, s32[52]{0:T(128)S(1)} %bitcast.153), kind=kOutput, calls=%fused_computation.14 | convolution fusion | flops 55053568 | bytes 1900752 | tf_op jit(solution)/shard_map/rfk,ft->rtk/dot_general | solution.py:34
  121.7 2.1 collective-permute-start.7
  123.8 40.5 %while.10 = (s32[]{:T(128)}, bf16[4,4,64,512]{3,2,1,0:T(8,128)(2,1)}, bf16[4,4,64,512]{3,2,1,0:T(8,128)(2,1)}, bf16[16,16]{1,0:T(8,128)(2,1)S(1)}, bf16[4,16,4,16]{3,1,2,0:T(8,128)(2,1)S(1)}, /*index=5*/s32[]{:T(128)}) while((s32[]{:T(128)}, bf16[4,4,64,512]{3,2,1,0:T(8,128)(2,1)}, bf16[4,4,64,512]{3,2,1,0:T(8,128)(2,1)}, ...), condition=%wide.region_1.2_spmd, body=%wide.region_0.1_spmd.sunk | while | flops 21233664 | bytes 4203593 | solution.py:66
  129.6 3.6 %broadcast_in_dim.31 = bf16[1,4,64,512]{3,2,1,0:T(8,128)(2,1)S(1)} reshape(bf16[4,16,4,32,16]{4,3,2,1,0:T(8,128)(2,1)S(1)} %copy.76) | data formatting | bytes 524288 | tf_op jit(solution)/shard_map/while/body/jit(dynamic_update_index_in_dim)/broadcast_in_dim | solution.py:66
  139.7 3.6 %broadcast_in_dim.31 = bf16[1,4,64,512]{3,2,1,0:T(8,128)(2,1)S(1)} reshape(bf16[4,16,4,32,16]{4,3,2,1,0:T(8,128)(2,1)S(1)} %copy.76) | data formatting | bytes 524288 | tf_op jit(solution)/shard_map/while/body/jit(dynamic_update_index_in_dim)/broadcast_in_dim | solution.py:66
  149.8 3.6 %broadcast_in_dim.31 = bf16[1,4,64,512]{3,2,1,0:T(8,128)(2,1)S(1)} reshape(bf16[4,16,4,32,16]{4,3,2,1,0:T(8,128)(2,1)S(1)} %copy.76) | data formatting | bytes 524288 | tf_op jit(solution)/shard_map/while/body/jit(dynamic_update_index_in_dim)/broadcast_in_dim | solution.py:66
  159.9 3.6 %broadcast_in_dim.31 = bf16[1,4,64,512]{3,2,1,0:T(8,128)(2,1)S(1)} reshape(bf16[4,16,4,32,16]{4,3,2,1,0:T(8,128)(2,1)S(1)} %copy.76) | data formatting | bytes 524288 | tf_op jit(solution)/shard_map/while/body/jit(dynamic_update_index_in_dim)/broadcast_in_dim | solution.py:66
  164.2 1.8 copy.59
  167.3 1.7 fusion.9
  169.0 1.9 collective-permute-start.10
  171.6 1.7 fusion.8
  173.3 1.9 collective-permute-start.9
  175.9 1.7 fusion.7
  177.6 3.7 %collective-permute-start.8 = (f32[16,16]{1,0:T(8,128)S(1)}, f32[16,16]{1,0:T(8,128)S(1)}, u32[]{:S(2)}, u32[]{:S(2)}) collective-permute-start(f32[16,16]{1,0:T(8,128)S(1)} %bitcast.151), channel_id=1, source_target_pairs={{4,0},{8,4},{12,8},{16,12},{20,16},{24,20},{28,24},{32,28},{36,32}... | collective-permute-start | bytes 3080 | tf_op jit(solution)/shard_map/ppermute | solution.py:16
  181.9 1.8 fusion.10
  183.8 1.9 collective-permute-start.11
  189.8 16.4 %collective-permute-done.11 = f32[16,16]{1,0:T(8,128)S(1)} collective-permute-done((f32[16,16]{1,0:T(8,128)S(1)}, f32[16,16]{1,0:T(8,128)S(1)}, u32[]{:S(2)}, u32[]{:S(2)}) %collective-permute-start.11) | collective-permute-done | bytes 1056 | tf_op jit(solution)/shard_map/ppermute | solution.py:16
  206.5 11.7 %all_to_all.25 = f32[4,1,576]{2,1,0:T(1,128)S(1)} all-to-all(f32[4,1,576]{2,1,0:T(1,128)S(1)} %reshape.136), channel_id=1, replica_groups=mesh['sta'=128,'cell'=4] {'cell'}, dimensions={0} | all-to-all | bytes 18432 | tf_op jit(solution)/shard_map/all_to_all | solution.py:26
  (90 shorter events, 42.6 us)
Async XLA Ops:
  0.0 68.3 %copy-start = (bf16[128,128]{1,0:T(8,128)(2,1)S(1)}, bf16[128,128]{1,0:T(8,128)(2,1)}, u32[]{:S(2)}) copy-start(bf16[128,128]{1,0:T(8,128)(2,1)} %param.15) | copy-start | bytes 98308
  0.0 61.5 %all-to-all-start = ((bf16[16,52,512]{2,0,1:T(8,128)(2,1)}), bf16[16,52,512]{2,0,1:T(8,128)(2,1)S(1)}, u32[]{:S(2)}, u32[]{:S(2)}) async-start(bf16[16,52,512]{2,0,1:T(8,128)(2,1)} %param.10), calls=%async_computation | async-start | bytes 1703936 | tf_op jit(solution)/shard_map/all_to_all | solution.py:81
  7.4 41.8 %collective-permute-start.4 = (bf16[16,52,512]{2,0,1:T(8,128)(2,1)}, bf16[16,52,512]{2,0,1:T(8,128)(2,1)S(1)}, u32[]{:S(2)}, u32[]{:S(2)}) collective-permute-start(bf16[16,52,512]{2,0,1:T(8,128)(2,1)} %param.10), channel_id=1, source_target_pairs={{508,0},{0,4},{4,8},{8,12},{12,16},{16,20},{20,24},{24,28},{28,32}... | collective-permute-start | bytes 2555912 | tf_op jit(solution)/shard_map/ppermute | solution.py:16
  9.3 13.9 %collective-permute-start = (s32[1,52]{1,0:T(1,128)}, s32[1,52]{1,0:T(1,128)S(1)}, u32[]{:S(2)}, u32[]{:S(2)}) collective-permute-start(s32[1,52]{1,0:T(1,128)} %param.11), channel_id=1, source_target_pairs={{508,0},{0,4},{4,8},{8,12},{12,16},{16,20},{20,24},{24,28},{28,32}... | collective-permute-start | bytes 632 | tf_op jit(solution)/shard_map/ppermute | solution.py:16
  23.3 10.2 %collective-permute-start.1 = (s32[1,52]{1,0:T(1,128)S(1)}, s32[1,52]{1,0:T(1,128)S(1)}, u32[]{:S(2)}, u32[]{:S(2)}) collective-permute-start(s32[1,52]{1,0:T(1,128)S(1)} %collective-permute-done), channel_id=1, source_target_pairs={{508,0},{0,4},{4,8},{8,12},{12,16},{16,20},{20,24},{24,28},{28,32}... | collective-permute-start | bytes 632 | tf_op jit(solution)/shard_map/ppermute | solution.py:16
  33.5 64.2 %collective-permute-start.2 = (s32[1,52]{1,0:T(1,128)S(1)}, s32[1,52]{1,0:T(1,128)S(1)}, u32[]{:S(2)}, u32[]{:S(2)}) collective-permute-start(s32[1,52]{1,0:T(1,128)S(1)} %collective-permute-done.1), channel_id=1, source_target_pairs={{508,0},{0,4},{4,8},{8,12},{12,16},{16,20},{20,24},{24,28},{28,32}... | collective-permute-start | bytes 632 | tf_op jit(solution)/shard_map/ppermute | solution.py:16
  49.2 19.1 %copy-start.4 = (bf16[16,52,512]{2,0,1:T(8,128)(2,1)}, bf16[16,52,512]{2,0,1:T(8,128)(2,1)S(1)}, u32[]{:S(2)}) copy-start(bf16[16,52,512]{2,0,1:T(8,128)(2,1)S(1)} %collective-permute-done.4) | copy-start | bytes 2555908
  49.2 50.5 %collective-permute-start.5 = (bf16[16,52,512]{2,0,1:T(8,128)(2,1)S(1)}, bf16[16,52,512]{2,0,1:T(8,128)(2,1)}, u32[]{:S(2)}, u32[]{:S(2)}) collective-permute-start(bf16[16,52,512]{2,0,1:T(8,128)(2,1)S(1)} %collective-permute-done.4), channel_id=1, source_target_pairs={{508,0},{0,4},{4,8},{8,12},{12,16},{16,20},{20,24},{24,28},{28,32}... | collective-permute-start | bytes 2555912 | tf_op jit(solution)/shard_map/ppermute | solution.py:16
  90.7 28.7 %copy-start.3 = (s32[1,52]{1,0:T(1,128)S(1)}, s32[1,52]{1,0:T(1,128)}, u32[]{:S(2)}) copy-start(s32[1,52]{1,0:T(1,128)} %param.11) | copy-start | bytes 628
  91.7 32.1 %copy-start.2 = (bf16[16,16]{1,0:T(8,128)(2,1)S(1)}, bf16[16,16]{1,0:T(8,128)(2,1)}, u32[]{:S(2)}) copy-start(bf16[16,16]{1,0:T(8,128)(2,1)} %param.13) | copy-start | bytes 1540
  91.7 27.7 %all-to-all-start.1 = ((bf16[4,16,13,512]{3,1,2,0:T(8,128)(2,1)}), bf16[4,16,13,512]{3,1,2,0:T(8,128)(2,1)S(1)}, u32[]{:S(2)}, u32[]{:S(2)}) async-start(bf16[4,16,13,512]{3,1,2,0:T(8,128)(2,1)} %pad_maximum_fusion), calls=%async_computation.1 | async-start | bytes 1703936 | tf_op jit(solution)/shard_map/all_to_all | solution.py:85
  97.7 4.9 %collective-permute-start.3 = (s32[1,52]{1,0:T(1,128)S(1)}, s32[1,52]{1,0:T(1,128)S(1)}, u32[]{:S(2)}, u32[]{:S(2)}) collective-permute-start(s32[1,52]{1,0:T(1,128)S(1)} %collective-permute-done.2), channel_id=1, source_target_pairs={{508,0},{0,4},{4,8},{8,12},{12,16},{16,20},{20,24},{24,28},{28,32}... | collective-permute-start | bytes 632 | tf_op jit(solution)/shard_map/ppermute | solution.py:16
  99.7 22.0 %collective-permute-start.6 = (bf16[16,52,512]{2,0,1:T(8,128)(2,1)}, bf16[16,52,512]{2,0,1:T(8,128)(2,1)}, u32[]{:S(2)}, u32[]{:S(2)}) collective-permute-start(bf16[16,52,512]{2,0,1:T(8,128)(2,1)} %collective-permute-done.5), channel_id=1, source_target_pairs={{508,0},{0,4},{4,8},{8,12},{12,16},{16,20},{20,24},{24,28},{28,32}... | collective-permute-start | bytes 2555912 | tf_op jit(solution)/shard_map/ppermute | solution.py:16
  121.7 60.2 %collective-permute-start.7 = (bf16[16,52,512]{2,0,1:T(8,128)(2,1)}, bf16[16,52,512]{2,0,1:T(8,128)(2,1)}, u32[]{:S(2)}, u32[]{:S(2)}) collective-permute-start(bf16[16,52,512]{2,0,1:T(8,128)(2,1)} %collective-permute-done.6), channel_id=1, source_target_pairs={{508,0},{0,4},{4,8},{8,12},{12,16},{16,20},{20,24},{24,28},{28,32}... | collective-permute-start | bytes 2555912 | tf_op jit(solution)/shard_map/ppermute | solution.py:16
  169.0 17.5 %collective-permute-start.10 = (f32[16,16]{1,0:T(8,128)S(1)}, f32[16,16]{1,0:T(8,128)S(1)}, u32[]{:S(2)}, u32[]{:S(2)}) collective-permute-start(f32[16,16]{1,0:T(8,128)S(1)} %bitcast.149), channel_id=1, source_target_pairs={{12,0},{16,4},{20,8},{24,12},{28,16},{32,20},{36,24},{40,28},{44,3... | collective-permute-start | bytes 3080 | tf_op jit(solution)/shard_map/ppermute | solution.py:16
  173.3 14.9 %collective-permute-start.9 = (f32[16,16]{1,0:T(8,128)S(1)}, f32[16,16]{1,0:T(8,128)S(1)}, u32[]{:S(2)}, u32[]{:S(2)}) collective-permute-start(f32[16,16]{1,0:T(8,128)S(1)} %bitcast.150), channel_id=1, source_target_pairs={{8,0},{12,4},{16,8},{20,12},{24,16},{28,20},{32,24},{36,28},{40,32... | collective-permute-start | bytes 3080 | tf_op jit(solution)/shard_map/ppermute | solution.py:16
  177.6 12.2 %collective-permute-start.8 = (f32[16,16]{1,0:T(8,128)S(1)}, f32[16,16]{1,0:T(8,128)S(1)}, u32[]{:S(2)}, u32[]{:S(2)}) collective-permute-start(f32[16,16]{1,0:T(8,128)S(1)} %bitcast.151), channel_id=1, source_target_pairs={{4,0},{8,4},{12,8},{16,12},{20,16},{24,20},{28,24},{32,28},{36,32}... | collective-permute-start | bytes 3080 | tf_op jit(solution)/shard_map/ppermute | solution.py:16
  181.9 3.8 %copy-start.1 = (bf16[16,52,512]{2,0,1:T(8,128)(2,1)S(1)}, bf16[16,52,512]{2,0,1:T(8,128)(2,1)}, u32[]{:S(2)}) copy-start(bf16[16,52,512]{2,0,1:T(8,128)(2,1)} %param.10) | copy-start | bytes 2555908
  183.8 22.4 %collective-permute-start.11 = (f32[16,16]{1,0:T(8,128)S(1)}, f32[16,16]{1,0:T(8,128)S(1)}, u32[]{:S(2)}, u32[]{:S(2)}) collective-permute-start(f32[16,16]{1,0:T(8,128)S(1)} %bitcast.152), channel_id=1, source_target_pairs={{16,0},{20,4},{24,8},{28,12},{32,16},{36,20},{40,24},{44,28},{48,3... | collective-permute-start | bytes 3080 | tf_op jit(solution)/shard_map/ppermute | solution.py:16
